TPU v7x, 128 devices: a whole 4x4x4 slice. The times are simulated.
128 devices in a mesh: row: 8 (over z_lo, y), col: 16 (over z_hi, x, core).
Axes of the slice: x: 4, y: 4, z: 4 (z_hi: 2, z_lo: 2; z = z_hi * 2 + z_lo), core: 2. Of those that a mesh axis runs over, the one named last changes fastest.
Arguments:
- observed: float32 [4, 65536], P(None, ('row', 'col')), may hold values from -50 to 50
- tile_values: bfloat16 [256, 32, 256, 256], P('row', 'col'), may hold values from -2.2649514 to 2.2649514
- tile_cols: int32 [256, 32], P('row', 'col'), may hold values from 0 to 255
Outputs:
- solution: float32 [4, 1048576], P(None, ('col', 'row'))
- residual_ratio: float32 [4], replicated
All inputs are finite; a program needn't handle non-finite values.
Results may differ from a plain program's by a relative error of at most 0.0021.
Values may be sent and summed in bfloat16 or wider, within the bound.
A program may use at most 128 MiB of HBM per device.

v0:
```python
import jax
import jax.numpy as jnp
from jax import lax
from jax.sharding import PartitionSpec as P

ITERS = 2
N = 1048576
epsilon_sq = 1e-06


def local(observed, tile_values, tile_cols):
    right_sides = observed.shape[0]
    row_tiles = tile_values.shape[0]
    per_block = tile_values.shape[1]
    tile_size = tile_values.shape[2]
    col_tiles = N // (tile_size * lax.axis_size("col"))
    panel_len = col_tiles * tile_size
    share_len = panel_len // lax.axis_size("row")
    flat_cols = tile_cols.reshape(-1)

    def adjoint_map(left_bf):
        gathered = lax.all_gather(left_bf, "col", axis=1, tiled=True).reshape(
            right_sides, row_tiles, tile_size
        )
        tile_terms = jnp.einsum(
            "rktj,nrt->nrkj", tile_values, gathered, preferred_element_type=jnp.float32
        )
        tile_terms = tile_terms.reshape(right_sides, row_tiles * per_block, tile_size)
        placed = (
            jnp.zeros((right_sides, col_tiles, tile_size), jnp.float32)
            .at[:, flat_cols]
            .add(tile_terms)
        )
        placed = placed.reshape(right_sides, panel_len)
        summed = lax.psum_scatter(placed, "row", scatter_dimension=1, tiled=True)
        return summed

    def lanczos_pair(left_raw, right_vec):
        beta_sq = lax.psum(jnp.sum(left_raw * left_raw, axis=1), ("row", "col"))
        beta_norm = jnp.sqrt(beta_sq + epsilon_sq)
        product = adjoint_map(left_raw.astype(jnp.bfloat16))
        right_raw = product / beta_norm[:, None] - beta_norm[:, None] * right_vec
        alpha_sq = lax.psum(jnp.sum(right_raw * right_raw, axis=1), ("row", "col"))
        alpha_norm = jnp.sqrt(alpha_sq + epsilon_sq)
        return (beta_norm, alpha_norm, right_raw)

    blank_right = jnp.zeros((right_sides, share_len), jnp.float32)
    beta_norm, alpha_norm, right_raw = lanczos_pair(observed, blank_right)
    first_beta = beta_norm
    left_vec = observed / beta_norm[:, None]
    right_vec = right_raw / alpha_norm[:, None]
    right_bf = right_raw.astype(jnp.bfloat16)
    phibar = beta_norm
    rhobar = alpha_norm
    direction = right_vec
    solution = jnp.zeros_like(right_vec)
    for iteration in range(ITERS):
        whole_panel = lax.all_gather(right_bf, "row", axis=1, tiled=True)
        picked = jnp.take(whole_panel.reshape(right_sides, col_tiles, tile_size), tile_cols, axis=1)
        partial_rows = jnp.einsum(
            "rktj,nrkj->nrt", tile_values, picked, preferred_element_type=jnp.float32
        )
        left_raw = (
            lax.psum_scatter(
                partial_rows.reshape(right_sides, row_tiles * tile_size),
                "col",
                scatter_dimension=1,
                tiled=True,
            )
            / alpha_norm[:, None]
            - alpha_norm[:, None] * left_vec
        )
        beta_norm, alpha_norm, right_raw = lanczos_pair(left_raw, right_vec)
        left_vec = left_raw / beta_norm[:, None]
        right_vec = right_raw / alpha_norm[:, None]
        right_bf = right_raw.astype(jnp.bfloat16)
        rho_val = jnp.sqrt(rhobar * rhobar + beta_norm * beta_norm)
        cosine = rhobar / rho_val
        sine_val = beta_norm / rho_val
        theta_val = sine_val * alpha_norm
        rhobar = -cosine * alpha_norm
        phi_val = cosine * phibar
        phibar = sine_val * phibar
        solution = solution + (phi_val / rho_val)[:, None] * direction
        direction = right_vec - (theta_val / rho_val)[:, None] * direction
    return (solution, phibar / first_beta)


def solution(mesh):
    in_specs = (P(None, ("row", "col")), P("row", "col", None, None), P("row", "col"))
    out_specs = (P(None, ("col", "row")), P())
    return jax.shard_map(local, mesh=mesh, in_specs=in_specs, out_specs=out_specs, check_vma=False)
```

profile of v0, /device:TPU:1, one launch (start us, length us, event | category | flops | bytes accessed | tf_op | source)
XLA Modules:
  0.0 1160.2 jit_solution(9524676217768432283)
XLA Ops:
  7.2 0.0 reduce-scatter.13.cloned.1.call-start
  7.2 0.9 fusion.20
  8.1 26.5 %all_gather.12 = bf16[4,8192]{1,0:T(4,128)(2,1)S(1)} all-gather(bf16[4,512]{1,0:T(4,128)(2,1)S(1)} %get-tuple-element.13), channel_id=1, replica_groups=mesh['row'=8,'col'=16] {'col'}, dimensions={1}, use_global_device_ids=true | all-gather | bytes 69632 | tf_op jit(solution)/shard_map/all_gather | solution.py:22
  34.6 0.8 copy.17
  35.4 0.1 reshape.77
  35.5 4.6 fusion.21
  40.0 0.1 broadcast.38.clone
  40.2 2.8 scatter_fusion
  43.0 16.1 %copy.26 = f32[4,65536]{0,1:T(8,128)} copy(f32[4,65536]{1,0:T(4,128)S(1)} %bitcast.65) | data formatting | bytes 2097152
  59.1 0.0 copy-start.1
  59.1 0.0 reduce-scatter.13.cloned.1.call-update
  59.1 0.0 reduce-scatter.15.cloned.1.call-start
  59.2 369.9 %psum.35 = f32[4]{0:T(128)S(1)} all-reduce(f32[4]{0:T(128)S(1)} %get-tuple-element.14), channel_id=1, replica_groups=mesh['row'=8,'col'=16] {'row','col'}, use_global_device_ids=true, to_apply=%region_3.0 | all-reduce | flops 4 | bytes 32 | tf_op jit(solution)/shard_map/psum | solution.py:39
  429.1 0.0 copy-done.1
  429.1 0.1 copy.19
  429.2 0.1 reshape.124
  429.3 0.1 copy.18
  429.4 0.0 reduce-scatter.13.cloned.1.call-done
  429.5 2.8 copy.27
  432.3 0.3 multiply_reduce_fusion.1
  432.6 22.8 %all_gather.13 = bf16[4,65536]{1,0:T(4,128)(2,1)S(1)} all-gather(bf16[4,8192]{1,0:T(4,128)(2,1)S(1)} %convert_element_type.13), channel_id=1, replica_groups=mesh['row'=8,'col'=16] {'row'}, dimensions={1}, use_global_device_ids=true | all-gather | bytes 589824 | tf_op jit(solution)/shard_map/all_gather | solution.py:58
  455.4 0.7 gather_fusion
  456.1 0.0 copy-start
  456.1 5.7 fusion.2
  461.8 2.6 copy.28
  464.4 0.0 reduce-scatter.15.cloned.1.call-update
  464.5 0.0 reduce-scatter.17.cloned.1.call-start
  464.5 74.8 %psum.36 = f32[4]{0:T(128)S(1)} all-reduce(f32[4]{0:T(128)S(1)} %get-tuple-element.11), channel_id=1, replica_groups=mesh['row'=8,'col'=16] {'row','col'}, use_global_device_ids=true, to_apply=%region_5.0 | all-reduce | flops 4 | bytes 32 | tf_op jit(solution)/shard_map/psum | solution.py:43
  539.4 8.0 reduce-scatter.15.cloned.1.call-done
  547.4 1.1 copy.29
  548.4 0.0 copy-done
  548.4 0.2 multiply_reduce_fusion.2
  548.7 23.2 %all_gather.14 = bf16[4,8192]{1,0:T(4,128)(2,1)S(1)} all-gather(bf16[4,512]{1,0:T(4,128)(2,1)S(1)} %convert_element_type.14), channel_id=1, replica_groups=mesh['row'=8,'col'=16] {'col'}, dimensions={1}, use_global_device_ids=true | all-gather | bytes 69632 | tf_op jit(solution)/shard_map/all_gather | solution.py:22
  571.8 4.6 fusion.22
  576.4 0.1 broadcast.38
  576.6 2.8 scatter_fusion.1
  579.4 16.1 %copy.30 = f32[4,65536]{0,1:T(8,128)} copy(f32[4,65536]{1,0:T(4,128)S(1)} %bitcast.64) | data formatting | bytes 2097152
  595.5 0.0 reduce-scatter.17.cloned.1.call-update
  595.5 0.0 reduce-scatter.19.cloned.1.call-start
  595.6 371.7 %psum.37 = f32[4]{0:T(128)S(1)} all-reduce(f32[4]{0:T(128)S(1)} %get-tuple-element.9), channel_id=1, replica_groups=mesh['row'=8,'col'=16] {'row','col'}, use_global_device_ids=true, to_apply=%region_8.10 | all-reduce | flops 4 | bytes 32 | tf_op jit(solution)/shard_map/psum | solution.py:39
  967.3 0.0 reduce-scatter.17.cloned.1.call-done
  967.3 2.8 copy.31
  970.2 0.1 fusion.19
  970.3 23.0 %all_gather.15 = bf16[4,65536]{1,0:T(4,128)(2,1)S(1)} all-gather(bf16[4,8192]{1,0:T(4,128)(2,1)S(1)} %get-tuple-element.7), channel_id=1, replica_groups=mesh['row'=8,'col'=16] {'row'}, dimensions={1}, use_global_device_ids=true | all-gather | bytes 589824 | tf_op jit(solution)/shard_map/all_gather | solution.py:58
  993.3 0.7 gather_fusion.1
  994.0 5.7 fusion
  999.7 2.6 copy.32
  1002.3 0.2 multiply_reduce_fusion
  1002.5 0.0 reduce-scatter.19.cloned.1.call-update
  1002.5 75.0 %psum.38 = f32[4]{0:T(128)S(1)} all-reduce(f32[4]{0:T(128)S(1)} %multiply_reduce_fusion), channel_id=1, replica_groups=mesh['row'=8,'col'=16] {'row','col'}, use_global_device_ids=true, to_apply=%region_12.14 | all-reduce | flops 4 | bytes 32 | tf_op jit(solution)/shard_map/psum | solution.py:43
  1077.5 8.0 reduce-scatter.19.cloned.1.call-done
  1085.5 1.1 copy.33
  1086.5 0.2 fusion.11
  1086.7 65.6 %psum.39 = f32[4]{0:T(128)S(1)} all-reduce(f32[4]{0:T(128)S(1)} %fusion.11), channel_id=1, replica_groups=mesh['row'=8,'col'=16] {'row','col'}, use_global_device_ids=true, to_apply=%region_15.17 | all-reduce | flops 4 | bytes 32 | tf_op jit(solution)/shard_map/psum | solution.py:39
  1152.3 0.6 multiply_divide_fusion
  1152.9 0.8 multiply_add_fusion
  (11 shorter events, 0.1 us)
Async XLA Ops:
  7.2 422.3 %reduce-scatter.13.cloned.1.call-start = ((), (), s32[]{:S(2)}) async-start(), calls=%async_computation.4 | async-start | bytes 37748736
  59.1 370.0 %copy-start.1 = (s32[32,2]{0,1:T(2,128)S(1)}, s32[32,2]{0,1:T(2,128)}, u32[]{:S(2)}) copy-start(s32[32,2]{0,1:T(2,128)} %param.7) | copy-start | bytes 772
  59.1 488.2 %reduce-scatter.15.cloned.1.call-start = ((), (), s32[]{:S(2)}) async-start(), calls=%async_computation.5 | async-start | bytes 4456448
  456.1 92.3 %copy-start = (f32[4,512]{1,0:T(4,128)S(1)}, f32[4,512]{1,0:T(4,128)}, u32[]{:S(2)}) copy-start(f32[4,512]{1,0:T(4,128)} %param.5) | copy-start | bytes 24580
  464.5 502.9 %reduce-scatter.17.cloned.1.call-start = ((), (), s32[]{:S(2)}) async-start(), calls=%async_computation.6 | async-start | bytes 37748736
  595.5 490.0 %reduce-scatter.19.cloned.1.call-start = ((), (), s32[]{:S(2)}) async-start(), calls=%async_computation.7 | async-start | bytes 4456448
Sparse Core Ops, SparseCore 0:
  59.3 325.6 reduce-scatter.12
  464.6 82.7 reduce-scatter.14
  595.6 327.5 reduce-scatter.16
  1002.6 82.7 reduce-scatter.18
where the time goes:
time: 1160 us
  blocking collectives  1050 us (91%)
  local copies, waits for them, and re-layouts  48 us (4%)
  matrix products  20.5 us (2%)
  waiting for transfers between devices  16.1 us (1%)
  between operations  13.9 us (1%)
    psum x3, blocking collectives, lanczos_pair(): beta_sq = lax.psum(jnp.sum(left_raw * left_raw, axis=1), ('row', 'col'))  807 us
    psum x2, blocking collectives, lanczos_pair(): alpha_sq = lax.psum(jnp.sum(right_raw * right_raw, axis=1), ('row', 'col'))  150 us
    all_gather x2, blocking collectives, adjoint_map(): lax.all_gather(left_bf, 'col', axis=1, tiled=True)  49.7 us
    unnamed x13, local copies, waits for them, and re-layouts  46 us
    all_gather x2, blocking collectives, local(): whole_panel = lax.all_gather(right_bf, 'row', axis=1, tiled=True)  45.8 us
  transfers between devices with their start and end apart: 4, of which 2 were waited for; matrix products, arithmetic and copies ran while one was open for 0% of the time, Pallas kernels for 0%

commit v1 on v0

--- a/solution.py
+++ b/solution.py
@@ -40,7 +40,8 @@
         beta_norm = jnp.sqrt(beta_sq + epsilon_sq)
         product = adjoint_map(left_raw.astype(jnp.bfloat16))
         right_raw = product / beta_norm[:, None] - beta_norm[:, None] * right_vec
-        alpha_sq = lax.psum(jnp.sum(right_raw * right_raw, axis=1), ("row", "col"))
+        tile_in = jnp.sum(right_raw * right_raw, axis=1)
+        alpha_sq = jax.lax.psum(jax.lax.psum(tile_in, "row"), axis_name="col")
         alpha_norm = jnp.sqrt(alpha_sq + epsilon_sq)
         return (beta_norm, alpha_norm, right_raw)
 

time: 1160 us -> 1190 us (1.026)
  waiting for transfers between devices: 16.1 us -> 85.8 us
  blocking collectives: 1050 us -> 1020 us
    unnamed x8, waiting for transfers between devices: 16.1 us -> 85.8 us
    psum x2 -> x4, blocking collectives: 150 us -> 113 us  [lanczos_pair(): alpha_sq = jax.lax.psum(jax.lax.psum(tile_in, 'row'), axis_name='col')]
where the time goes in v1:
time: 1190 us
  blocking collectives  1020 us (86%)
  waiting for transfers between devices  85.8 us (7%)
  local copies, waits for them, and re-layouts  48 us (4%)
  matrix products  20.5 us (2%)
  between operations  13.9 us (1%)
    psum x3, blocking collectives, lanczos_pair(): beta_sq = lax.psum(jnp.sum(left_raw * left_raw, axis=1), ('row', 'col'))  808 us
    psum x4, blocking collectives, lanczos_pair(): alpha_sq = jax.lax.psum(jax.lax.psum(tile_in, 'row'), axis_name='col')  113 us
    unnamed x8, waiting for transfers between devices  85.8 us
    all_gather x2, blocking collectives, adjoint_map(): lax.all_gather(left_bf, 'col', axis=1, tiled=True)  49.6 us
    unnamed x13, local copies, waits for them, and re-layouts  46 us
    all_gather x2, blocking collectives, local(): whole_panel = lax.all_gather(right_bf, 'row', axis=1, tiled=True)  45.8 us
  transfers between devices with their start and end apart: 4, of which 2 were waited for; matrix products, arithmetic and copies ran while one was open for 0% of the time, Pallas kernels for 0%

profile of v1, /device:TPU:1, one launch (start us, length us, event | category | flops | bytes accessed | tf_op | source)
XLA Modules:
  0.0 1193.8 jit_solution(7008680737794645352)
XLA Ops:
  7.2 0.0 reduce-scatter.13.cloned.1.call-start
  7.2 0.9 fusion.20
  8.1 26.5 %all_gather.12 = bf16[4,8192]{1,0:T(4,128)(2,1)S(1)} all-gather(bf16[4,512]{1,0:T(4,128)(2,1)S(1)} %get-tuple-element.13), channel_id=1, replica_groups=mesh['row'=8,'col'=16] {'col'}, dimensions={1}, use_global_device_ids=true | all-gather | bytes 69632 | tf_op jit(solution)/shard_map/all_gather | solution.py:22
  34.6 0.8 copy.17
  35.4 0.1 reshape.77
  35.5 4.6 fusion.21
  40.0 0.1 broadcast.38.clone
  40.2 2.8 scatter_fusion
  43.0 16.1 %copy.26 = f32[4,65536]{0,1:T(8,128)} copy(f32[4,65536]{1,0:T(4,128)S(1)} %bitcast.65) | data formatting | bytes 2097152
  59.1 0.0 copy-start.1
  59.1 0.0 reduce-scatter.13.cloned.1.call-update
  59.1 0.0 reduce-scatter.15.cloned.1.call-start
  59.2 369.9 %psum.49 = f32[4]{0:T(128)S(1)} all-reduce(f32[4]{0:T(128)S(1)} %get-tuple-element.14), channel_id=1, replica_groups=mesh['row'=8,'col'=16] {'row','col'}, use_global_device_ids=true, to_apply=%region_3.0 | all-reduce | flops 4 | bytes 32 | tf_op jit(solution)/shard_map/psum | solution.py:39
  429.1 0.0 copy-done.1
  429.1 0.1 copy.19
  429.2 0.1 reshape.124
  429.3 0.1 copy.18
  429.4 0.0 reduce-scatter.13.cloned.1.call-done
  429.5 2.8 copy.27
  432.3 0.3 multiply_reduce_fusion.1
  432.6 22.8 %all_gather.13 = bf16[4,65536]{1,0:T(4,128)(2,1)S(1)} all-gather(bf16[4,8192]{1,0:T(4,128)(2,1)S(1)} %convert_element_type.13), channel_id=1, replica_groups=mesh['row'=8,'col'=16] {'row'}, dimensions={1}, use_global_device_ids=true | all-gather | bytes 589824 | tf_op jit(solution)/shard_map/all_gather | solution.py:59
  455.4 0.7 gather_fusion
  456.1 0.0 copy-start
  456.1 5.7 fusion.2
  461.8 2.6 copy.28
  464.4 14.0 %psum.50 = f32[4]{0:T(128)S(1)} all-reduce(f32[4]{0:T(128)S(1)} %get-tuple-element.11), channel_id=1, replica_groups=mesh['row'=8,'col'=16] {'row'}, use_global_device_ids=true, to_apply=%region_5.0 | all-reduce | flops 4 | bytes 32 | tf_op jit(solution)/shard_map/psum | solution.py:44
  478.5 0.0 reduce-scatter.15.cloned.1.call-update
  478.5 0.0 reduce-scatter.17.cloned.1.call-start
  478.5 42.6 %psum.51 = f32[4]{0:T(128)S(1)} all-reduce(f32[4]{0:T(128)S(1)} %psum.50), channel_id=1, replica_groups=mesh['row'=8,'col'=16] {'col'}, use_global_device_ids=true, to_apply=%region_6.0 | all-reduce | flops 4 | bytes 32 | tf_op jit(solution)/shard_map/psum | solution.py:44
  521.1 42.8 %reduce-scatter.15.cloned.1.call-done = f32[512,4]{1,0:T(8,128)} async-done(((f32[8192,4]{1,0:T(8,128)}), f32[512,4]{1,0:T(8,128)}) %reduce-scatter.15.cloned.1.call-update) | async-done | bytes 8208
  563.9 1.1 copy.29
  565.0 0.0 copy-done
  565.0 0.2 multiply_reduce_fusion.2
  565.2 23.1 %all_gather.14 = bf16[4,8192]{1,0:T(4,128)(2,1)S(1)} all-gather(bf16[4,512]{1,0:T(4,128)(2,1)S(1)} %convert_element_type.14), channel_id=1, replica_groups=mesh['row'=8,'col'=16] {'col'}, dimensions={1}, use_global_device_ids=true | all-gather | bytes 69632 | tf_op jit(solution)/shard_map/all_gather | solution.py:22
  588.3 4.6 fusion.22
  592.9 0.1 broadcast.38
  593.1 2.8 scatter_fusion.1
  595.9 16.1 %copy.30 = f32[4,65536]{0,1:T(8,128)} copy(f32[4,65536]{1,0:T(4,128)S(1)} %bitcast.64) | data formatting | bytes 2097152
  612.0 0.0 reduce-scatter.17.cloned.1.call-update
  612.0 0.0 reduce-scatter.19.cloned.1.call-start
  612.1 372.1 %psum.52 = f32[4]{0:T(128)S(1)} all-reduce(f32[4]{0:T(128)S(1)} %get-tuple-element.9), channel_id=1, replica_groups=mesh['row'=8,'col'=16] {'row','col'}, use_global_device_ids=true, to_apply=%region_9.11 | all-reduce | flops 4 | bytes 32 | tf_op jit(solution)/shard_map/psum | solution.py:39
  984.1 0.0 reduce-scatter.17.cloned.1.call-done
  984.1 2.8 copy.31
  987.0 0.1 fusion.19
  987.1 23.0 %all_gather.15 = bf16[4,65536]{1,0:T(4,128)(2,1)S(1)} all-gather(bf16[4,8192]{1,0:T(4,128)(2,1)S(1)} %get-tuple-element.7), channel_id=1, replica_groups=mesh['row'=8,'col'=16] {'row'}, dimensions={1}, use_global_device_ids=true | all-gather | bytes 589824 | tf_op jit(solution)/shard_map/all_gather | solution.py:59
  1010.1 0.7 gather_fusion.1
  1010.8 5.7 fusion
  1016.5 0.2 multiply_reduce_fusion
  1016.7 2.6 copy.32
  1019.3 14.0 %psum.53 = f32[4]{0:T(128)S(1)} all-reduce(f32[4]{0:T(128)S(1)} %multiply_reduce_fusion), channel_id=1, replica_groups=mesh['row'=8,'col'=16] {'row'}, use_global_device_ids=true, to_apply=%region_13.15 | all-reduce | flops 4 | bytes 32 | tf_op jit(solution)/shard_map/psum | solution.py:44
  1033.3 0.0 reduce-scatter.19.cloned.1.call-update
  1033.4 42.6 %psum.54 = f32[4]{0:T(128)S(1)} all-reduce(f32[4]{0:T(128)S(1)} %psum.53), channel_id=1, replica_groups=mesh['row'=8,'col'=16] {'col'}, use_global_device_ids=true, to_apply=%region_14.16 | all-reduce | flops 4 | bytes 32 | tf_op jit(solution)/shard_map/psum | solution.py:44
  1075.9 42.9 %reduce-scatter.19.cloned.1.call-done = f32[512,4]{1,0:T(8,128)} async-done(((f32[8192,4]{1,0:T(8,128)}), f32[512,4]{1,0:T(8,128)}) %reduce-scatter.19.cloned.1.call-update) | async-done | bytes 8208
  1118.9 1.1 copy.33
  1119.9 0.2 fusion.11
  1120.1 65.7 %psum.55 = f32[4]{0:T(128)S(1)} all-reduce(f32[4]{0:T(128)S(1)} %fusion.11), channel_id=1, replica_groups=mesh['row'=8,'col'=16] {'row','col'}, use_global_device_ids=true, to_apply=%region_17.19 | all-reduce | flops 4 | bytes 32 | tf_op jit(solution)/shard_map/psum | solution.py:39
  1185.8 0.6 multiply_divide_fusion
  1186.4 0.8 multiply_add_fusion
  (11 shorter events, 0.1 us)
Async XLA Ops:
  7.2 422.3 %reduce-scatter.13.cloned.1.call-start = ((), (), s32[]{:S(2)}) async-start(), calls=%async_computation.4 | async-start | bytes 37748736
  59.1 370.0 %copy-start.1 = (s32[32,2]{0,1:T(2,128)S(1)}, s32[32,2]{0,1:T(2,128)}, u32[]{:S(2)}) copy-start(s32[32,2]{0,1:T(2,128)} %param.7) | copy-start | bytes 772
  59.1 504.8 %reduce-scatter.15.cloned.1.call-start = ((), (), s32[]{:S(2)}) async-start(), calls=%async_computation.5 | async-start | bytes 4456448
  456.1 108.9 %copy-start = (f32[4,512]{1,0:T(4,128)S(1)}, f32[4,512]{1,0:T(4,128)}, u32[]{:S(2)}) copy-start(f32[4,512]{1,0:T(4,128)} %param.5) | copy-start | bytes 24580
  478.5 505.6 %reduce-scatter.17.cloned.1.call-start = ((), (), s32[]{:S(2)}) async-start(), calls=%async_computation.6 | async-start | bytes 37748736
  612.0 506.9 %reduce-scatter.19.cloned.1.call-start = ((), (), s32[]{:S(2)}) async-start(), calls=%async_computation.7 | async-start | bytes 4456448
Sparse Core Ops, SparseCore 0:
  59.3 325.6 reduce-scatter.12
  478.6 85.2 reduce-scatter.14
  612.1 327.8 reduce-scatter.16
  1033.5 85.3 reduce-scatter.18
